TPU v7x, 32 devices: a whole 2x2x4 slice. The times are simulated.
32 devices in a mesh: kv: 2 (over x), seq: 16 (over z, y, core).
Axes of the slice: x: 2, y: 2, z: 4, core: 2. Of those that a mesh axis runs over, the one named last changes fastest.
Arguments:
- hidden: bfloat16 [1024, 2048], P('seq', 'kv'), may hold values from -1.5 to 1.5
- in_gain: float32 [2048], replicated, may hold values from 0.5 to 1.5
- w_query: bfloat16 [2048, 2048], P(None, 'kv'), may hold values from -0.125 to 0.125
- key_projection_weight: bfloat16 [2048, 1024], P(None, 'kv'), may hold values from -0.125 to 0.125
- value_projection_weight: bfloat16 [2048, 1024], P(None, 'kv'), may hold values from -0.125 to 0.125
- w_gate: bfloat16 [2048, 16], P(None, 'kv'), may hold values from -0.125 to 0.125
- w_out: bfloat16 [2048, 2048], P('kv'), may hold values from -0.125 to 0.125
- q_gain: float32 [128], replicated, may hold values from 0.1 to 1.9
- k_gain: float32 [128], replicated, may hold values from 0.1 to 1.9
- cache_keys: bfloat16 [32768, 8, 128], P('seq', 'kv'), may hold values from -160 to 160
- pooled_cache_values: bfloat16 [32768, 8, 128], P('seq', 'kv'), may hold values from -6 to 6
- prefix_len: int32 [4], replicated, may hold values from 1024 to 8192, as said below
- own_len: int32 [32], replicated, may hold values from 256 to 2048, as said below
- request_group: int32 [32], replicated, may hold values from 0 to 3, as said below
- parents: int32 [32, 32], P('seq'), may hold values from 0 to 30, as said below
- accepted_leaf: int32 [32], P('seq'), may hold values from 0 to 31
Outputs:
- layer_out: bfloat16 [1024, 2048], P('seq', 'kv')
- accepted_keys: bfloat16 [32, 32, 1024], P('seq', None, 'kv')
- accepted_values: bfloat16 [32, 32, 1024], P('seq', None, 'kv')
Inputs may be any that keep to these rules, and one draw needn't show every extreme that they name: parents[r, 0] is 0 and node 0 is the root; for i >= 1, parents[r, i] < i. `prefix_len`: the lengths sum to 32768 // 2; one is exactly 8192 and one exactly 1024. `own_len`: the lengths sum to 32768 // 2; one is exactly 2048 and one exactly 256. `request_group`: every group holds exactly 8 requests.
All inputs are finite; a program needn't handle non-finite values.
Results may differ from a plain program's by a relative error of at most 0.017.
The roundings to bfloat16 on the way count: a program that leaves them out, or rounds other values in their place, can miss the bound.
Values may be sent and summed in bfloat16 or wider, within the bound.
A program may use at most 128 MiB of HBM per device.

v0:
```python
import math
import jax
import jax.numpy as jnp
from jax import lax
from jax.sharding import PartitionSpec as P

EPSILON = 1e-06
ROPE_BASE = 1000000.0
NEGATIVE = -1e30


def rms_scale(values, scales):
    mean_square = jnp.mean(values * values, axis=-1, keepdims=True)
    return values * lax.rsqrt(mean_square + EPSILON) * scales


def rotate_pairs(values, positions):
    half_width = values.shape[-1] // 2
    freqs = jnp.exp(
        jnp.arange(half_width, dtype=jnp.float32) * (-2.0 * math.log(ROPE_BASE) / values.shape[-1])
    )
    angles = positions[:, None] * freqs[None, :]
    cosine = jnp.concatenate([jnp.cos(angles), jnp.cos(angles)], axis=-1)[:, None, :]
    sine = jnp.concatenate([jnp.sin(angles), jnp.sin(angles)], axis=-1)[:, None, :]
    turned = jnp.concatenate([-values[..., half_width:], values[..., :half_width]], axis=-1)
    return values * cosine + turned * sine


def tree_paths(parents):
    width = parents.shape[-1]
    nodes = jnp.arange(width, dtype=jnp.int32)
    linked = (parents[:, :, None] == nodes[None, None, :]).astype(jnp.float32)
    identity_mat = jnp.eye(width, dtype=jnp.float32)
    reach = jnp.minimum(identity_mat[None] + linked * (1.0 - identity_mat[None]), 1.0)
    for squaring in range(max(1, (width - 1).bit_length())):
        reach = jnp.minimum(
            jnp.einsum("mij,mjk->mik", reach, reach, precision=lax.Precision.HIGHEST), 1.0
        )
    depth_f = jnp.sum(reach, axis=-1) - 1.0
    return (reach, depth_f)


def accepted_rows(reach, depth_f, leaves, tree_rows):
    width = reach.shape[-1]
    nodes = jnp.arange(width, dtype=jnp.int32)
    leaf_pick = (leaves[:, None] == nodes[None, :]).astype(jnp.float32)
    on_path = jnp.einsum("mi,mij->mj", leaf_pick, reach, precision=lax.Precision.HIGHEST)
    levels = (depth_f[:, None, :] == nodes.astype(jnp.float32)[None, :, None]).astype(jnp.float32)
    select = levels * on_path[:, None, :]
    return jnp.einsum(
        "mdj,mjc->mdc", select, tree_rows.astype(jnp.float32), precision=lax.Precision.HIGHEST
    ).astype(jnp.bfloat16)


def body(
    hidden,
    in_gain,
    w_query,
    key_projection_weight,
    value_projection_weight,
    w_gate,
    w_out,
    q_gain,
    k_gain,
    cache_keys,
    pooled_cache_values,
    prefix_len,
    own_len,
    request_group,
    parents,
    accepted_leaf,
):
    local_req, tree = parents.shape
    groups = prefix_len.shape[0]
    requests = own_len.shape[0]
    head_width = q_gain.shape[0]
    local_heads = w_gate.shape[1]
    local_kv = key_projection_weight.shape[1] // head_width
    per_kv = local_heads // local_kv
    local_tok = hidden.shape[0]
    pool_dev = cache_keys.shape[0]
    seq_index = lax.axis_index("seq")
    score_scale = 1.0 / math.sqrt(head_width)
    full_rows = lax.all_gather(hidden, "kv", axis=1, tiled=True)
    normed = rms_scale(full_rows.astype(jnp.float32), in_gain).astype(jnp.bfloat16)
    reach, depth_f = tree_paths(parents)
    all_reqs = jnp.arange(requests, dtype=jnp.int32)
    my_reqs = seq_index * local_req + jnp.arange(local_req, dtype=jnp.int32)
    my_pick = (my_reqs[:, None] == all_reqs[None, :]).astype(jnp.int32)
    my_group = jnp.sum(my_pick * request_group[None, :], axis=1)
    group_ids = jnp.arange(groups, dtype=jnp.int32)
    group_pick = (my_group[:, None] == group_ids[None, :]).astype(jnp.int32)
    context = jnp.sum(group_pick * prefix_len[None, :], axis=1) + jnp.sum(
        my_pick * own_len[None, :], axis=1
    )
    positions = (context[:, None].astype(jnp.float32) + depth_f).reshape(-1)
    query = jnp.dot(normed, w_query, preferred_element_type=jnp.float32).reshape(
        local_tok, local_heads, head_width
    )
    query = rotate_pairs(rms_scale(query, q_gain), positions).astype(jnp.bfloat16)
    key_new = jnp.dot(normed, key_projection_weight, preferred_element_type=jnp.float32).reshape(
        local_tok, local_kv, head_width
    )
    key_new = rotate_pairs(rms_scale(key_new, k_gain), positions).astype(jnp.bfloat16)
    value_new = (
        jnp.dot(normed, value_projection_weight, preferred_element_type=jnp.float32)
        .astype(jnp.bfloat16)
        .reshape(local_tok, local_kv, head_width)
    )
    gate_logit = jnp.dot(normed, w_gate, preferred_element_type=jnp.float32)
    tree_query = query.reshape(local_req, tree, local_kv, per_kv, head_width)
    tree_keys = key_new.reshape(local_req, tree, local_kv, head_width)
    tree_values = value_new.reshape(local_req, tree, local_kv, head_width)
    tree_scores = (
        jnp.einsum("atkgd,askd->atkgs", tree_query, tree_keys, preferred_element_type=jnp.float32)
        * score_scale
    )
    tree_seen = (reach > 0.5)[:, :, None, None, :]
    tree_scores = jnp.where(tree_seen, tree_scores, NEGATIVE)
    tree_max = jnp.max(tree_scores, axis=-1)
    tree_weights = jnp.where(tree_seen, jnp.exp(tree_scores - tree_max[..., None]), 0.0)
    tree_sum = jnp.sum(tree_weights, axis=-1).reshape(local_tok, local_heads)
    tree_num = jnp.einsum(
        "atkgs,askd->atkgd",
        tree_weights.astype(jnp.bfloat16),
        tree_values,
        preferred_element_type=jnp.float32,
    ).reshape(local_tok, local_heads, head_width)
    tree_max = tree_max.reshape(local_tok, local_heads)
    lengths_all = jnp.concatenate([prefix_len, own_len])
    starts = jnp.cumsum(lengths_all) - lengths_all
    slot_ids = seq_index * pool_dev + jnp.arange(pool_dev, dtype=jnp.int32)
    slot_segment = jnp.sum((starts[None, :] <= slot_ids[:, None]).astype(jnp.int32), axis=1) - 1
    block_len = min(512, pool_dev)
    block_count = pool_dev // block_len
    key_blocks = cache_keys.reshape(block_count, block_len, local_kv, head_width)
    value_blocks = pooled_cache_values.reshape(block_count, block_len, local_kv, head_width)
    segment_blocks = slot_segment.reshape(block_count, block_len)
    query_flat = query.reshape(local_tok, local_heads * head_width)
    query_piece = lax.all_gather(query_flat, "seq", axis=0, tiled=True)
    row_ids = jnp.arange(query_piece.shape[0], dtype=jnp.int32)
    owners = row_ids // tree
    count = query_piece.shape[0]
    grouped = query_piece.reshape(count, local_kv, per_kv, head_width)
    owner_pick = (owners[:, None] == all_reqs[None, :]).astype(jnp.int32)
    known = owners >= 0
    prefix_segment = jnp.where(known, jnp.sum(owner_pick * request_group[None, :], axis=1), -5)
    own_segment = jnp.where(known, owners + groups, -5)

    def visit(carry, block):
        run_max, run_sum, run_num = carry
        keys_block, values_block, segment_block = block
        scores = (
            jnp.einsum("nkgd,pkd->nkgp", grouped, keys_block, preferred_element_type=jnp.float32)
            * score_scale
        )
        visible = (segment_block[None, :] == prefix_segment[:, None]) | (
            segment_block[None, :] == own_segment[:, None]
        )
        visible = visible[:, None, None, :]
        scores = jnp.where(visible, scores, NEGATIVE)
        new_max = jnp.maximum(run_max, jnp.max(scores, axis=-1))
        weights = jnp.where(visible, jnp.exp(scores - new_max[..., None]), 0.0)
        factor = jnp.exp(run_max - new_max)
        run_sum = run_sum * factor + jnp.sum(weights, axis=-1)
        run_num = run_num * factor[..., None] + jnp.einsum(
            "nkgp,pkd->nkgd",
            weights.astype(jnp.bfloat16),
            values_block,
            preferred_element_type=jnp.float32,
        )
        return ((new_max, run_sum, run_num), None)

    start_state = (
        jnp.full((count, local_kv, per_kv), NEGATIVE, jnp.float32),
        jnp.zeros((count, local_kv, per_kv), jnp.float32),
        jnp.zeros((count, local_kv, per_kv, head_width), jnp.float32),
    )
    final_state, unused = lax.scan(visit, start_state, (key_blocks, value_blocks, segment_blocks))
    run_max, run_sum, run_num = final_state
    part_max = run_max.reshape(count, local_heads)
    part_sum = run_sum.reshape(count, local_heads)
    part_num = run_num.reshape(count, local_heads * head_width)
    all_rows = part_max.shape[0]
    cache_max = lax.pmax(part_max.astype(jnp.bfloat16), "seq").astype(part_max.dtype)
    factor = jnp.exp(part_max - cache_max)
    scaled_num = (part_num.reshape(all_rows, local_heads, head_width) * factor[..., None]).reshape(
        all_rows, local_heads * head_width
    )
    summed_num, summed_sum = (
        lax.psum_scatter(
            scaled_num.astype(jnp.bfloat16), "seq", scatter_dimension=0, tiled=True
        ).astype(jnp.float32),
        lax.psum_scatter(
            (part_sum * factor).astype(jnp.bfloat16), "seq", scatter_dimension=0, tiled=True
        ).astype(jnp.float32),
    )
    own_max = lax.dynamic_slice_in_dim(cache_max, seq_index * local_tok, local_tok, 0)
    final_max = jnp.maximum(own_max, tree_max)
    cache_factor = jnp.exp(own_max - final_max)
    tree_factor = jnp.exp(tree_max - final_max)
    weight_sum = summed_sum * cache_factor + tree_sum * tree_factor
    mixed = (
        summed_num.reshape(local_tok, local_heads, head_width) * cache_factor[..., None]
        + tree_num * tree_factor[..., None]
    )
    mixed = mixed / weight_sum[..., None]
    attended = (
        (mixed * jax.nn.sigmoid(gate_logit)[..., None])
        .astype(jnp.bfloat16)
        .reshape(local_tok, local_heads * head_width)
    )
    projected = jnp.dot(attended, w_out, preferred_element_type=jnp.float32)
    layer_part = lax.psum_scatter(
        projected.astype(jnp.bfloat16), "kv", scatter_dimension=1, tiled=True
    ).astype(jnp.float32)
    layer_out = (layer_part + hidden.astype(jnp.float32)).astype(jnp.bfloat16)
    tree_rows = jnp.concatenate(
        [
            key_new.reshape(local_req, tree, local_kv * head_width),
            value_new.reshape(local_req, tree, local_kv * head_width),
        ],
        axis=-1,
    )
    picked = accepted_rows(reach, depth_f, accepted_leaf, tree_rows)
    accepted_keys = picked[:, :, : local_kv * head_width]
    accepted_values = picked[:, :, local_kv * head_width :]
    return (layer_out, accepted_keys, accepted_values)


def solution(mesh):
    in_specs = (
        P("seq", "kv"),
        P(),
        P(None, "kv"),
        P(None, "kv"),
        P(None, "kv"),
        P(None, "kv"),
        P("kv", None),
        P(),
        P(),
        P("seq", "kv", None),
        P("seq", "kv", None),
        P(),
        P(),
        P(),
        P("seq", None),
        P("seq"),
    )
    out_specs = (P("seq", "kv"), P("seq", None, "kv"), P("seq", None, "kv"))
    return jax.shard_map(body, mesh=mesh, in_specs=in_specs, out_specs=out_specs, check_vma=False)
```

profile of v0, /device:TPU:0, one launch (start us, length us, event | category | flops | bytes accessed | tf_op | source)
XLA Modules:
  0.0 365.4 jit_solution(637547949621892404)
XLA Ops:
  8.1 7.4 %all_gather.6 = bf16[64,2048]{1,0:T(8,128)(2,1)S(1)} all-gather(bf16[64,1024]{1,0:T(8,128)(2,1)} %param.18), channel_id=1, replica_groups=mesh['kv'=2,'seq'=16] {'kv'}, dimensions={1}, use_global_device_ids=true | all-gather | bytes 393216 | tf_op jit(solution)/shard_map/all_gather | solution.py:84
  15.6 3.1 fusion.96
  26.7 39.9 %all-gather.2.cloned.1.call-done = bf16[1024,1024]{1,0:T(8,128)(2,1)} async-done(((bf16[64,1024]{1,0:T(8,128)(2,1)}), bf16[1024,1024]{1,0:T(8,128)(2,1)}) %all-gather.2.cloned.1.call-update) | async-done | bytes 2097168 | tf_op jit(solution)/shard_map/all_gather | solution.py:140
  66.6 4.5 %reshape.343 = bf16[1024,4,2,128]{3,2,1,0:T(2,128)(2,1)} reshape(bf16[1024,1024]{1,0:T(8,128)(2,1)} %all-gather.2.cloned.1.call-done) | data formatting | bytes 4194304 | tf_op jit(solution)/shard_map/reshape | solution.py:144
  71.1 3.2 copy.172
  74.3 84.1 %while.15 = (s32[]{:T(128)}, f32[1024,4,2]{0,2,1:T(2,128)S(1)}, f32[1024,4,2]{0,2,1:T(2,128)S(1)}, f32[1024,4,2,128]{0,3,2,1:T(8,128)}, s32[4,512]{1,0:T(4,128)S...) while((s32[]{:T(128)}, f32[1024,4,2]{0,2,1:T(2,128)S(1)}, ...), condition=%wide.region_12.13_spmd.clone, body=%wide.region_9.12_spmd.clone.sunk | while | flops 2206780416 | bytes 69748896 | solution.py:179
  74.7 2.4 constant_dynamic-slice_fusion.6
  78.2 4.6 %fusion.137 = (f32[1024,4,2]{0,2,1:T(2,128)S(1)}, f32[4,512,1024,2]{2,1,3,0:T(8,128)S(1)}) fusion(pred[1024,512]{0,1:T(8,128)(4,1)S(1)} %compare_or_fusion.2, bf16[1024,4,2,128]{3,0,2,1:T(8,128)(2,1)} %get-tuple-element.291, bf16[1,512,4,128]{3,2,1,0:T(4,128)(2,1)} %get-tuple-element.256), kind=kOutput, calls=%fused_computation.3.clone.1 | convolution fusion | flops 1086316544 | bytes 19955712 | tf_op jit(solution)/shard_map/while/body/eval_jaxpr/nkgd,pkd->nkgp/dot_general | solution.py:154
  82.8 4.1 %fusion.139 = f32[1024,4,2]{0,2,1:T(2,128)S(1)} fusion(f32[4,512,1024,2]{2,1,3,0:T(8,128)S(1)} %get-tuple-element.258, f32[1024,4,2]{0,2,1:T(2,128)S(1)} %fusion.138, pred[1024,512]{0,1:T(8,128)(4,1)S(1)} %compare_or_fusion.2), kind=kLoop, calls=%fused_computation.5.clone.1 | loop fusion | flops 20963328 | bytes 17367040 | tf_op jit(solution)/shard_map/while/body/eval_jaxpr/reduce_sum | solution.py:165
  87.0 7.1 %bitcast_add_fusion.2 = f32[1024,4,2,128]{0,3,2,1:T(8,128)} fusion(f32[1024,4,2,128]{0,3,2,1:T(8,128)} %get-tuple-element.276, f32[4,512,1024,2]{2,1,3,0:T(8,128)S(1)} %get-tuple-element.258, f32[1024,4,2]{0,2,1:T(2,128)S(1)} %fusion.138, pred[1024,512]{0,1:T(8,128)(4,1)S(1)} %compare_or_fusion.2, f32[1024,4,2]{0,2,1:T(2,128)S(1)} %get-tuple-element.260, ...), kind=kOutput, calls=%fused_computation.8.clone.1 | convolution fusion | flops 1097859072 | bytes 26279936 | tf_op jit(solution)/shard_map/while/body/eval_jaxpr/nkgp,pkd->nkgd/dot_general | solution.py:166
  94.6 2.4 constant_dynamic-slice_fusion.6
  98.1 4.6 %fusion.137 = (f32[1024,4,2]{0,2,1:T(2,128)S(1)}, f32[4,512,1024,2]{2,1,3,0:T(8,128)S(1)}) fusion(pred[1024,512]{0,1:T(8,128)(4,1)S(1)} %compare_or_fusion.2, bf16[1024,4,2,128]{3,0,2,1:T(8,128)(2,1)} %get-tuple-element.291, bf16[1,512,4,128]{3,2,1,0:T(4,128)(2,1)} %get-tuple-element.256), kind=kOutput, calls=%fused_computation.3.clone.1 | convolution fusion | flops 1086316544 | bytes 19955712 | tf_op jit(solution)/shard_map/while/body/eval_jaxpr/nkgd,pkd->nkgp/dot_general | solution.py:154
  102.7 4.1 %fusion.139 = f32[1024,4,2]{0,2,1:T(2,128)S(1)} fusion(f32[4,512,1024,2]{2,1,3,0:T(8,128)S(1)} %get-tuple-element.258, f32[1024,4,2]{0,2,1:T(2,128)S(1)} %fusion.138, pred[1024,512]{0,1:T(8,128)(4,1)S(1)} %compare_or_fusion.2), kind=kLoop, calls=%fused_computation.5.clone.1 | loop fusion | flops 20963328 | bytes 17367040 | tf_op jit(solution)/shard_map/while/body/eval_jaxpr/reduce_sum | solution.py:165
  106.9 8.7 %bitcast_add_fusion.2 = f32[1024,4,2,128]{0,3,2,1:T(8,128)} fusion(f32[1024,4,2,128]{0,3,2,1:T(8,128)} %get-tuple-element.276, f32[4,512,1024,2]{2,1,3,0:T(8,128)S(1)} %get-tuple-element.258, f32[1024,4,2]{0,2,1:T(2,128)S(1)} %fusion.138, pred[1024,512]{0,1:T(8,128)(4,1)S(1)} %compare_or_fusion.2, f32[1024,4,2]{0,2,1:T(2,128)S(1)} %get-tuple-element.260, ...), kind=kOutput, calls=%fused_computation.8.clone.1 | convolution fusion | flops 1097859072 | bytes 26279936 | tf_op jit(solution)/shard_map/while/body/eval_jaxpr/nkgp,pkd->nkgd/dot_general | solution.py:166
  116.0 2.4 constant_dynamic-slice_fusion.6
  119.5 4.6 %fusion.137 = (f32[1024,4,2]{0,2,1:T(2,128)S(1)}, f32[4,512,1024,2]{2,1,3,0:T(8,128)S(1)}) fusion(pred[1024,512]{0,1:T(8,128)(4,1)S(1)} %compare_or_fusion.2, bf16[1024,4,2,128]{3,0,2,1:T(8,128)(2,1)} %get-tuple-element.291, bf16[1,512,4,128]{3,2,1,0:T(4,128)(2,1)} %get-tuple-element.256), kind=kOutput, calls=%fused_computation.3.clone.1 | convolution fusion | flops 1086316544 | bytes 19955712 | tf_op jit(solution)/shard_map/while/body/eval_jaxpr/nkgd,pkd->nkgp/dot_general | solution.py:154
  124.1 4.1 %fusion.139 = f32[1024,4,2]{0,2,1:T(2,128)S(1)} fusion(f32[4,512,1024,2]{2,1,3,0:T(8,128)S(1)} %get-tuple-element.258, f32[1024,4,2]{0,2,1:T(2,128)S(1)} %fusion.138, pred[1024,512]{0,1:T(8,128)(4,1)S(1)} %compare_or_fusion.2), kind=kLoop, calls=%fused_computation.5.clone.1 | loop fusion | flops 20963328 | bytes 17367040 | tf_op jit(solution)/shard_map/while/body/eval_jaxpr/reduce_sum | solution.py:165
  128.3 8.7 %bitcast_add_fusion.2 = f32[1024,4,2,128]{0,3,2,1:T(8,128)} fusion(f32[1024,4,2,128]{0,3,2,1:T(8,128)} %get-tuple-element.276, f32[4,512,1024,2]{2,1,3,0:T(8,128)S(1)} %get-tuple-element.258, f32[1024,4,2]{0,2,1:T(2,128)S(1)} %fusion.138, pred[1024,512]{0,1:T(8,128)(4,1)S(1)} %compare_or_fusion.2, f32[1024,4,2]{0,2,1:T(2,128)S(1)} %get-tuple-element.260, ...), kind=kOutput, calls=%fused_computation.8.clone.1 | convolution fusion | flops 1097859072 | bytes 26279936 | tf_op jit(solution)/shard_map/while/body/eval_jaxpr/nkgp,pkd->nkgd/dot_general | solution.py:166
  137.4 2.4 constant_dynamic-slice_fusion.6
  140.9 4.6 %fusion.137 = (f32[1024,4,2]{0,2,1:T(2,128)S(1)}, f32[4,512,1024,2]{2,1,3,0:T(8,128)S(1)}) fusion(pred[1024,512]{0,1:T(8,128)(4,1)S(1)} %compare_or_fusion.2, bf16[1024,4,2,128]{3,0,2,1:T(8,128)(2,1)} %get-tuple-element.291, bf16[1,512,4,128]{3,2,1,0:T(4,128)(2,1)} %get-tuple-element.256), kind=kOutput, calls=%fused_computation.3.clone.1 | convolution fusion | flops 1086316544 | bytes 19955712 | tf_op jit(solution)/shard_map/while/body/eval_jaxpr/nkgd,pkd->nkgp/dot_general | solution.py:154
  145.5 4.1 %fusion.139 = f32[1024,4,2]{0,2,1:T(2,128)S(1)} fusion(f32[4,512,1024,2]{2,1,3,0:T(8,128)S(1)} %get-tuple-element.258, f32[1024,4,2]{0,2,1:T(2,128)S(1)} %fusion.138, pred[1024,512]{0,1:T(8,128)(4,1)S(1)} %compare_or_fusion.2), kind=kLoop, calls=%fused_computation.5.clone.1 | loop fusion | flops 20963328 | bytes 17367040 | tf_op jit(solution)/shard_map/while/body/eval_jaxpr/reduce_sum | solution.py:165
  149.7 8.7 %bitcast_add_fusion.2 = f32[1024,4,2,128]{0,3,2,1:T(8,128)} fusion(f32[1024,4,2,128]{0,3,2,1:T(8,128)} %get-tuple-element.276, f32[4,512,1024,2]{2,1,3,0:T(8,128)S(1)} %get-tuple-element.258, f32[1024,4,2]{0,2,1:T(2,128)S(1)} %fusion.138, pred[1024,512]{0,1:T(8,128)(4,1)S(1)} %compare_or_fusion.2, f32[1024,4,2]{0,2,1:T(2,128)S(1)} %get-tuple-element.260, ...), kind=kOutput, calls=%fused_computation.8.clone.1 | convolution fusion | flops 1097859072 | bytes 26279936 | tf_op jit(solution)/shard_map/while/body/eval_jaxpr/nkgp,pkd->nkgd/dot_general | solution.py:166
  158.4 5.4 %copy.208 = f32[1024,1024]{1,0:T(8,128)} copy(f32[1024,1024]{0,1:T(8,128)} %bitcast.172) | data formatting | bytes 8388608 | tf_op jit(solution)/shard_map/reshape;reshape | solution.py:187
  163.8 59.5 %pmax.7 = bf16[1024,8]{0,1:T(8,128)(2,1)S(1)} all-reduce(bf16[1024,8]{0,1:T(8,128)(2,1)S(1)} %convert_element_type.109), channel_id=1, replica_groups=mesh['kv'=2,'seq'=16] {'seq'}, use_global_device_ids=true, to_apply=%region_13.14 | all-reduce | flops 8192 | bytes 32768 | tf_op jit(solution)/shard_map/pmax | solution.py:185
  226.9 2.2 fusion.23
  232.1 1.4 copy.176
  236.3 2.1 convolution_convert_fusion.2
  251.4 25.6 %reduce-scatter.10.cloned.1.call-done = bf16[64,8]{1,0:T(8,128)(2,1)} async-done(((bf16[1024,8]{1,0:T(8,128)(2,1)}), bf16[64,8]{1,0:T(8,128)(2,1)}) %reduce-scatter.10.cloned.1.call-update) | async-done | bytes 1040
  278.1 63.2 %reduce-scatter.6.cloned.1.call-done = bf16[64,1024]{1,0:T(8,128)(2,1)} async-done(((bf16[1024,1024]{1,0:T(8,128)(2,1)}), bf16[64,1024]{1,0:T(8,128)(2,1)}) %reduce-scatter.6.cloned.1.call-update) | async-done | bytes 131088 | tf_op jit(solution)/shard_map/reduce_scatter | solution.py:191
  342.6 3.9 %convolution_convert_fusion = bf16[64,2048]{1,0:T(8,128)(2,1)} fusion(bf16[1024,2048]{1,0:T(8,128)(2,1)} %param.24, f32[8,8,8,128]{3,2,1,0:T(8,128)S(1)} %bitcast.180, f32[8,8,8,128]{3,2,1,0:T(8,128)S(1)} %bitcast.183, f32[64,1024]{1,0:T(8,128)S(1)} %reshape.350, f32[8,8,8,128]{3,2,1,0:T(8,128)S(1)} %bitcast.181, f32[8,8,8,128]{3,2,1,0:T(8,128)S(1)} %bitcast.182, ...), kind=kOutput, calls=%fused_computation.37 | convolution fusion | flops 269025280 | bytes 5898240 | tf_op jit(solution)/shard_map/dot_general | solution.py:213
  347.5 9.8 %reduce-scatter.8.cloned.1.call-done = bf16[64,1024]{1,0:T(8,128)(2,1)} async-done(((bf16[64,2048]{1,0:T(8,128)(2,1)}), bf16[64,1024]{1,0:T(8,128)(2,1)}) %reduce-scatter.8.cloned.1.call-update) | async-done | bytes 131088 | tf_op jit(solution)/shard_map/reduce_scatter | solution.py:214
  357.3 1.6 add_convert_fusion
  (207 shorter events, 40.8 us)
Async XLA Ops:
  7.2 17.1 %copy-start = (bf16[2048,512]{1,0:T(8,128)(2,1)S(1)}, bf16[2048,512]{1,0:T(8,128)(2,1)}, u32[]{:S(2)}) copy-start(bf16[2048,512]{1,0:T(8,128)(2,1)} %param.21) | copy-start | bytes 6291460
  7.2 11.9 %copy-start.21 = (f32[128]{0:T(128)S(1)}, f32[128]{0:T(128)}, u32[]{:S(2)}) copy-start(f32[128]{0:T(128)} %param.25) | copy-start | bytes 1540
  7.2 12.1 %copy-start.28 = (s32[2,32]{1,0:T(2,128)S(1)}, s32[2,32]{1,0:T(2,128)}, u32[]{:S(2)}) copy-start(s32[2,32]{1,0:T(2,128)} %param.32) | copy-start | bytes 772
  7.2 13.1 %copy-start.27 = (s32[32]{0:T(128)S(1)}, s32[32]{0:T(128)}, u32[]{:S(2)}) copy-start(s32[32]{0:T(128)} %param.30) | copy-start | bytes 388
  7.2 13.1 %copy-start.26 = (s32[32]{0:T(128)S(1)}, s32[32]{0:T(128)}, u32[]{:S(2)}) copy-start(s32[32]{0:T(128)} %param.31) | copy-start | bytes 388
  7.2 13.3 %copy-start.29 = (s32[4]{0:T(128)S(1)}, s32[4]{0:T(128)}, u32[]{:S(2)}) copy-start(s32[4]{0:T(128)} %param.29) | copy-start | bytes 52
  7.2 59.4 %all-gather.2.cloned.1.call-start = ((), (), s32[]{:S(2)}) async-start(), calls=%async_computation.3 | async-start | bytes 2228224 | tf_op jit(solution)/shard_map/all_gather | solution.py:140
  7.3 14.6 %copy-start.25 = (f32[64]{0:T(128)}, f32[64]{0:T(128)S(1)}, u32[]{:S(2)}) copy-start(f32[64]{0:T(128)S(1)} %multiply_exponential_fusion) | copy-start | bytes 772
  15.5 10.3 %copy-start.3 = (bf16[64,2048]{1,0:T(8,128)(2,1)}, bf16[64,2048]{1,0:T(8,128)(2,1)S(1)}, u32[]{:S(2)}) copy-start(bf16[64,2048]{1,0:T(8,128)(2,1)S(1)} %all_gather.6) | copy-start | bytes 786436
  15.6 10.2 %copy-start.22 = (f32[64]{0:T(128)}, f32[64]{0:T(128)S(1)}, u32[]{:S(2)}) copy-start(f32[64]{0:T(128)S(1)} %add_rsqrt_fusion.2) | copy-start | bytes 772
  15.6 8.6 %copy-start.19 = (f32[2048]{0:T(1024)S(1)}, f32[2048]{0:T(1024)}, u32[]{:S(2)}) copy-start(f32[2048]{0:T(1024)} %param.19) | copy-start | bytes 24580
  18.8 7.1 %copy-start.30 = (bf16[2048,8]{0,1:T(8,128)(2,1)S(1)}, bf16[2048,8]{0,1:T(8,128)(2,1)}, u32[]{:S(2)}) copy-start(bf16[2048,8]{0,1:T(8,128)(2,1)} %param.23) | copy-start | bytes 98308
  20.3 50.7 %copy-start.15 = (f32[2,32,32]{2,1,0:T(8,128)}, f32[2,32,32]{2,1,0:T(8,128)S(1)}, u32[]{:S(2)}) copy-start(f32[2,32,32]{2,1,0:T(8,128)S(1)} %get-tuple-element.190) | copy-start | bytes 24580
  21.3 49.8 %copy-start.24 = (f32[2,32]{1,0:T(2,128)}, f32[2,32]{1,0:T(2,128)S(1)}, u32[]{:S(2)}) copy-start(f32[2,32]{1,0:T(2,128)S(1)} %get-tuple-element.186) | copy-start | bytes 772
  23.6 253.4 %reduce-scatter.10.cloned.1.call-start = ((), (), s32[]{:S(2)}) async-start(), calls=%async_computation.6 | async-start | bytes 278528
  24.8 49.5 %copy-start.5 = (f32[64,512]{1,0:T(8,128)}, f32[64,512]{1,0:T(8,128)S(1)}, u32[]{:S(2)}) copy-start(f32[64,512]{1,0:T(8,128)S(1)} %fusion.94) | copy-start | bytes 393220
  82.8 4.2 %copy-start.2 = (bf16[1,512,4,128]{1,3,2,0:T(8,128)(2,1)S(1)}, bf16[1,512,4,128]{1,3,2,0:T(8,128)(2,1)}, u32[]{:S(2)}) copy-start(bf16[1,512,4,128]{1,3,2,0:T(8,128)(2,1)} %copy.285) | copy-start | bytes 1572868 | tf_op jit(solution)/shard_map/while
  102.7 4.2 %copy-start.2 = (bf16[1,512,4,128]{1,3,2,0:T(8,128)(2,1)S(1)}, bf16[1,512,4,128]{1,3,2,0:T(8,128)(2,1)}, u32[]{:S(2)}) copy-start(bf16[1,512,4,128]{1,3,2,0:T(8,128)(2,1)} %copy.285) | copy-start | bytes 1572868 | tf_op jit(solution)/shard_map/while
  124.1 4.2 %copy-start.2 = (bf16[1,512,4,128]{1,3,2,0:T(8,128)(2,1)S(1)}, bf16[1,512,4,128]{1,3,2,0:T(8,128)(2,1)}, u32[]{:S(2)}) copy-start(bf16[1,512,4,128]{1,3,2,0:T(8,128)(2,1)} %copy.285) | copy-start | bytes 1572868 | tf_op jit(solution)/shard_map/while
  145.5 4.2 %copy-start.2 = (bf16[1,512,4,128]{1,3,2,0:T(8,128)(2,1)S(1)}, bf16[1,512,4,128]{1,3,2,0:T(8,128)(2,1)}, u32[]{:S(2)}) copy-start(bf16[1,512,4,128]{1,3,2,0:T(8,128)(2,1)} %copy.285) | copy-start | bytes 1572868 | tf_op jit(solution)/shard_map/while
  224.2 117.1 %reduce-scatter.6.cloned.1.call-start = ((), (), s32[]{:S(2)}) async-start(), calls=%async_computation.4 | async-start | bytes 2228224 | tf_op jit(solution)/shard_map/reduce_scatter | solution.py:191
  224.7 2.2 copy-start.1
  226.9 3.6 copy-start.6
  226.9 9.5 %copy-start.4 = (bf16[64,2048]{1,0:T(8,128)(2,1)S(1)}, bf16[64,2048]{1,0:T(8,128)(2,1)}, u32[]{:S(2)}) copy-start(bf16[64,2048]{1,0:T(8,128)(2,1)} %copy-done.3) | copy-start | bytes 786436
  229.0 14.5 %copy-start.8 = (f32[64,8,64]{2,0,1:T(8,128)S(1)}, f32[64,8,64]{2,0,1:T(8,128)}, u32[]{:S(2)}) copy-start(f32[64,8,64]{2,0,1:T(8,128)} %copy-done.7) | copy-start | bytes 393220
  229.0 14.5 %copy-start.10 = (f32[64,8,64]{2,0,1:T(8,128)S(1)}, f32[64,8,64]{2,0,1:T(8,128)}, u32[]{:S(2)}) copy-start(f32[64,8,64]{2,0,1:T(8,128)} %copy-done.9) | copy-start | bytes 393220
  229.0 128.3 %reduce-scatter.8.cloned.1.call-start = ((), (), s32[]{:S(2)}) async-start(), calls=%async_computation.5 | async-start | bytes 393216 | tf_op jit(solution)/shard_map/reduce_scatter | solution.py:214
  229.1 2.1 copy-start.20
  232.1 9.6 %copy-start.17 = (f32[64,128]{1,0:T(8,128)S(1)}, f32[64,128]{1,0:T(8,128)}, u32[]{:S(2)}) copy-start(f32[64,128]{1,0:T(8,128)} %copy-done.16) | copy-start | bytes 98308
  247.1 99.4 %copy-start.12 = (bf16[64,512]{1,0:T(8,128)(2,1)S(1)}, bf16[64,512]{1,0:T(8,128)(2,1)}, u32[]{:S(2)}) copy-start(bf16[64,512]{1,0:T(8,128)(2,1)} %copy-done.11) | copy-start | bytes 196612
  247.1 99.4 %copy-start.23 = (f32[2,32]{1,0:T(2,128)S(1)}, f32[2,32]{1,0:T(2,128)}, u32[]{:S(2)}) copy-start(f32[2,32]{1,0:T(2,128)} %get-tuple-element.185) | copy-start | bytes 772
  251.4 105.9 %copy-start.13 = (bf16[64,1024]{1,0:T(8,128)(2,1)S(1)}, bf16[64,1024]{1,0:T(8,128)(2,1)}, u32[]{:S(2)}) copy-start(bf16[64,1024]{1,0:T(8,128)(2,1)} %param.18) | copy-start | bytes 393220
  (6 other events, 5.1 us)
Sparse Core Ops, SparseCore 0:
  23.7 42.8 all-gather.1
  224.3 52.5 reduce-scatter.9
  280.7 60.5 reduce-scatter.5
  346.6 10.6 reduce-scatter.7
where the time goes:
time: 367 us; the launch traced here: 365 us
  waiting for transfers between devices  139 us (38%)
  blocking collectives  66.8 us (18%)
  matrix products  66.7 us (18%)
  local copies, waits for them, and re-layouts  47.5 us (13%)
  other arithmetic  30.8 us (8%)
  between operations  14.5 us (4%)
    reduce_scatter x1, waiting for transfers between devices, body(): lax.psum_scatter(scaled_num.astype(jnp.bfloat16), 'seq', scatter_dimensio...  63.2 us
    pmax x1, blocking collectives, body(): lax.pmax(part_max.astype(jnp.bfloat16), 'seq').astype(part_max.dtype)  59.5 us
    all_gather x1, waiting for transfers between devices, body(): query_piece = lax.all_gather(query_flat, 'seq', axis=0, tiled=True)  39.9 us
    dot_general x4, matrix products, visit(): jnp.einsum('nkgp,pkd->nkgd', weights.astype(jnp.bfloat16), values_block,...  33.2 us
    unnamed x5, waiting for transfers between devices  25.6 us
    dot_general x4, matrix products, visit(): jnp.einsum('nkgd,pkd->nkgp', grouped, keys_block, preferred_element_type=...  18.3 us
    reduce_sum x4, other arithmetic, visit(): run_sum = run_sum * factor + jnp.sum(weights, axis=-1)  16.3 us
    dynamic_slice x12, local copies, waits for them, and re-layouts, body(): lax.scan(visit, start_state, (key_blocks, value_blocks, segment_blocks))  14 us
  transfers between devices with their start and end apart: 4, of which 4 were waited for; matrix products, arithmetic and copies ran while one was open for 8% of the time, Pallas kernels for 0%

commit v1 on v0

--- a/solution.py
+++ b/solution.py
@@ -137,7 +137,12 @@
     value_blocks = pooled_cache_values.reshape(block_count, block_len, local_kv, head_width)
     segment_blocks = slot_segment.reshape(block_count, block_len)
     query_flat = query.reshape(local_tok, local_heads * head_width)
-    query_piece = lax.all_gather(query_flat, "seq", axis=0, tiled=True)
+    ring = [query_flat]
+    for hop in range(15):
+        ring.append(lax.ppermute(ring[-1], "seq", [(dev, (dev + 1) % 16) for dev in range(16)]))
+    query_piece = jnp.roll(
+        jnp.concatenate(ring[::-1], axis=0), (lax.axis_index("seq") + 1) * ring[0].shape[0], axis=0
+    )
     row_ids = jnp.arange(query_piece.shape[0], dtype=jnp.int32)
     owners = row_ids // tree
     count = query_piece.shape[0]

time: 367 us -> 430 us (1.17)
  waiting for transfers between devices: 139 us -> 215 us
  local copies, waits for them, and re-layouts: 47.5 us -> 39.2 us
    ppermute x0 -> x15, waiting for transfers between devices: none -> 99.2 us  [body(): lax.ppermute(ring[-1], 'seq', [(dev, (dev + 1) % 16) for dev in range(16)])]
    all_gather x1 -> x0, waiting for transfers between devices: 39.9 us -> none  [body(): query_piece = lax.all_gather(query_flat, 'seq', axis=0, tiled=True)]
    unnamed x5 -> x4, waiting for transfers between devices: 25.6 us -> 42.3 us
    reshape x1 -> x0, local copies, waits for them, and re-layouts: 4.48 us -> none  [body(): grouped = query_piece.reshape(count, local_kv, per_kv, head_width)]
    unnamed x66 -> x117, local copies, waits for them, and re-layouts: 8.05 us -> 11.2 us
  transfers between devices with their start and end apart: 4 -> 18, of which waited for: 4 -> 18; matrix products, arithmetic and copies ran while one was open for 8% -> 4% of each run, Pallas kernels for 0% -> 0%
where the time goes in v1:
time: 430 us; the launch traced here: 429 us
  waiting for transfers between devices  215 us (50%)
  matrix products  65.2 us (15%)
  blocking collectives  65 us (15%)
  local copies, waits for them, and re-layouts  39.2 us (9%)
  other arithmetic  29.2 us (7%)
  between operations  14.9 us (3%)
    ppermute x15, waiting for transfers between devices, body(): lax.ppermute(ring[-1], 'seq', [(dev, (dev + 1) % 16) for dev in range(16)])  99.2 us
    reduce_scatter x1, waiting for transfers between devices, body(): lax.psum_scatter(scaled_num.astype(jnp.bfloat16), 'seq', scatter_dimensio...  63.3 us
    pmax x1, blocking collectives, body(): lax.pmax(part_max.astype(jnp.bfloat16), 'seq').astype(part_max.dtype)  57.6 us
    unnamed x4, waiting for transfers between devices  42.3 us
    dot_general x4, matrix products, visit(): jnp.einsum('nkgp,pkd->nkgd', weights.astype(jnp.bfloat16), values_block,...  33.3 us
    dot_general x4, matrix products, visit(): jnp.einsum('nkgd,pkd->nkgp', grouped, keys_block, preferred_element_type=...  17.3 us
    reduce_sum x4, other arithmetic, visit(): run_sum = run_sum * factor + jnp.sum(weights, axis=-1)  16.3 us
    dynamic_slice x12, local copies, waits for them, and re-layouts, body(): lax.scan(visit, start_state, (key_blocks, value_blocks, segment_blocks))  14 us
  transfers between devices with their start and end apart: 18, of which 18 were waited for; matrix products, arithmetic and copies ran while one was open for 4% of the time, Pallas kernels for 0%

profile of v1, /device:TPU:0, one launch (start us, length us, event | category | flops | bytes accessed | tf_op | source)
XLA Modules:
  0.0 428.8 jit_solution(6113868158757689058)
XLA Ops:
  8.1 7.4 %all_gather.3 = bf16[64,2048]{1,0:T(8,128)(2,1)S(1)} all-gather(bf16[64,1024]{1,0:T(8,128)(2,1)} %param.18), channel_id=1, replica_groups=mesh['kv'=2,'seq'=16] {'kv'}, dimensions={1}, use_global_device_ids=true | all-gather | bytes 393216 | tf_op jit(solution)/shard_map/all_gather | solution.py:84
  23.1 7.1 %collective-permute-done = bf16[64,1024]{1,0:T(8,128)(2,1)S(1)} collective-permute-done((bf16[64,1024]{1,0:T(8,128)(2,1)S(1)}, bf16[64,1024]{1,0:T(8,128)(2,1)S(1)}, u32[]{:S(2)}, u32[]{:S(2)}) %collective-permute-start) | collective-permute-done | bytes 131104 | tf_op jit(solution)/shard_map/ppermute | solution.py:142
  30.2 7.1 %collective-permute-done.1 = bf16[64,1024]{1,0:T(8,128)(2,1)S(1)} collective-permute-done((bf16[64,1024]{1,0:T(8,128)(2,1)S(1)}, bf16[64,1024]{1,0:T(8,128)(2,1)S(1)}, u32[]{:S(2)}, u32[]{:S(2)}) %collective-permute-start.1) | collective-permute-done | bytes 131104 | tf_op jit(solution)/shard_map/ppermute | solution.py:142
  37.3 7.1 %collective-permute-done.2 = bf16[64,1024]{1,0:T(8,128)(2,1)S(1)} collective-permute-done((bf16[64,1024]{1,0:T(8,128)(2,1)S(1)}, bf16[64,1024]{1,0:T(8,128)(2,1)S(1)}, u32[]{:S(2)}, u32[]{:S(2)}) %collective-permute-start.2) | collective-permute-done | bytes 131104 | tf_op jit(solution)/shard_map/ppermute | solution.py:142
  44.4 7.1 %collective-permute-done.3 = bf16[64,1024]{1,0:T(8,128)(2,1)S(1)} collective-permute-done((bf16[64,1024]{1,0:T(8,128)(2,1)S(1)}, bf16[64,1024]{1,0:T(8,128)(2,1)S(1)}, u32[]{:S(2)}, u32[]{:S(2)}) %collective-permute-start.3) | collective-permute-done | bytes 131104 | tf_op jit(solution)/shard_map/ppermute | solution.py:142
  51.5 7.1 %collective-permute-done.4 = bf16[64,1024]{1,0:T(8,128)(2,1)S(1)} collective-permute-done((bf16[64,1024]{1,0:T(8,128)(2,1)S(1)}, bf16[64,1024]{1,0:T(8,128)(2,1)S(1)}, u32[]{:S(2)}, u32[]{:S(2)}) %collective-permute-start.4) | collective-permute-done | bytes 131104 | tf_op jit(solution)/shard_map/ppermute | solution.py:142
  58.6 7.1 %collective-permute-done.5 = bf16[64,1024]{1,0:T(8,128)(2,1)S(1)} collective-permute-done((bf16[64,1024]{1,0:T(8,128)(2,1)S(1)}, bf16[64,1024]{1,0:T(8,128)(2,1)S(1)}, u32[]{:S(2)}, u32[]{:S(2)}) %collective-permute-start.5) | collective-permute-done | bytes 131104 | tf_op jit(solution)/shard_map/ppermute | solution.py:142
  65.7 7.1 %collective-permute-done.6 = bf16[64,1024]{1,0:T(8,128)(2,1)S(1)} collective-permute-done((bf16[64,1024]{1,0:T(8,128)(2,1)S(1)}, bf16[64,1024]{1,0:T(8,128)(2,1)S(1)}, u32[]{:S(2)}, u32[]{:S(2)}) %collective-permute-start.6) | collective-permute-done | bytes 131104 | tf_op jit(solution)/shard_map/ppermute | solution.py:142
  75.2 4.8 %collective-permute-done.7 = bf16[64,1024]{1,0:T(8,128)(2,1)} collective-permute-done((bf16[64,1024]{1,0:T(8,128)(2,1)S(1)}, bf16[64,1024]{1,0:T(8,128)(2,1)}, u32[]{:S(2)}, u32[]{:S(2)}) %collective-permute-start.7) | collective-permute-done | bytes 131104 | tf_op jit(solution)/shard_map/ppermute | solution.py:142
  81.7 5.7 %collective-permute-done.8 = bf16[64,1024]{1,0:T(8,128)(2,1)S(1)} collective-permute-done((bf16[64,1024]{1,0:T(8,128)(2,1)}, bf16[64,1024]{1,0:T(8,128)(2,1)S(1)}, u32[]{:S(2)}, u32[]{:S(2)}) %collective-permute-start.8) | collective-permute-done | bytes 131104 | tf_op jit(solution)/shard_map/ppermute | solution.py:142
  88.7 5.7 %collective-permute-done.9 = bf16[64,1024]{1,0:T(8,128)(2,1)S(1)} collective-permute-done((bf16[64,1024]{1,0:T(8,128)(2,1)S(1)}, bf16[64,1024]{1,0:T(8,128)(2,1)S(1)}, u32[]{:S(2)}, u32[]{:S(2)}) %collective-permute-start.9) | collective-permute-done | bytes 131104 | tf_op jit(solution)/shard_map/ppermute | solution.py:142
  95.2 6.3 %collective-permute-done.10 = bf16[64,1024]{1,0:T(8,128)(2,1)S(1)} collective-permute-done((bf16[64,1024]{1,0:T(8,128)(2,1)S(1)}, bf16[64,1024]{1,0:T(8,128)(2,1)S(1)}, u32[]{:S(2)}, u32[]{:S(2)}) %collective-permute-start.10) | collective-permute-done | bytes 131104 | tf_op jit(solution)/shard_map/ppermute | solution.py:142
  101.6 7.0 %collective-permute-done.11 = bf16[64,1024]{1,0:T(8,128)(2,1)S(1)} collective-permute-done((bf16[64,1024]{1,0:T(8,128)(2,1)S(1)}, bf16[64,1024]{1,0:T(8,128)(2,1)S(1)}, u32[]{:S(2)}, u32[]{:S(2)}) %collective-permute-start.11) | collective-permute-done | bytes 131104 | tf_op jit(solution)/shard_map/ppermute | solution.py:142
  108.8 6.9 %collective-permute-done.12 = bf16[64,1024]{1,0:T(8,128)(2,1)S(1)} collective-permute-done((bf16[64,1024]{1,0:T(8,128)(2,1)S(1)}, bf16[64,1024]{1,0:T(8,128)(2,1)S(1)}, u32[]{:S(2)}, u32[]{:S(2)}) %collective-permute-start.12) | collective-permute-done | bytes 131104 | tf_op jit(solution)/shard_map/ppermute | solution.py:142
  116.6 6.2 %collective-permute-done.13 = bf16[64,1024]{1,0:T(8,128)(2,1)S(1)} collective-permute-done((bf16[64,1024]{1,0:T(8,128)(2,1)S(1)}, bf16[64,1024]{1,0:T(8,128)(2,1)S(1)}, u32[]{:S(2)}, u32[]{:S(2)}) %collective-permute-start.13) | collective-permute-done | bytes 131104 | tf_op jit(solution)/shard_map/ppermute | solution.py:142
  122.8 7.1 %collective-permute-done.14 = bf16[64,1024]{1,0:T(8,128)(2,1)S(1)} collective-permute-done((bf16[64,1024]{1,0:T(8,128)(2,1)S(1)}, bf16[64,1024]{1,0:T(8,128)(2,1)S(1)}, u32[]{:S(2)}, u32[]{:S(2)}) %collective-permute-start.14) | collective-permute-done | bytes 131104 | tf_op jit(solution)/shard_map/ppermute | solution.py:142
  140.8 83.2 %while.15 = (s32[]{:T(128)}, f32[1024,4,2]{0,2,1:T(2,128)S(1)}, f32[1024,4,2]{0,2,1:T(2,128)S(1)}, f32[1024,4,2,128]{0,3,2,1:T(8,128)}, s32[4,512]{1,0:T(4,128)S...) while((s32[]{:T(128)}, f32[1024,4,2]{0,2,1:T(2,128)S(1)}, ...), condition=%wide.region_12.13_spmd.clone, body=%wide.region_9.12_spmd.clone.sunk | while | flops 2206780416 | bytes 69748896 | solution.py:184
  144.8 4.3 %fusion.137 = (f32[1024,4,2]{0,2,1:T(2,128)S(1)}, f32[4,512,1024,2]{2,1,3,0:T(8,128)S(1)}) fusion(pred[1024,512]{0,1:T(8,128)(4,1)S(1)} %compare_or_fusion.2, bf16[1024,4,2,128]{3,0,2,1:T(8,128)(2,1)S(1)} %get-tuple-element.282, bf16[1,512,4,128]{3,2,1,0:T(4,128)(2,1)} %get-tuple-element.247), kind=kOutput, calls=%fused_computation.3.clone.1 | convolution fusion | flops 1086316544 | bytes 19955712 | tf_op jit(solution)/shard_map/while/body/eval_jaxpr/nkgd,pkd->nkgp/dot_general | solution.py:159
  153.3 7.2 %bitcast_add_fusion.2 = f32[1024,4,2,128]{0,3,2,1:T(8,128)} fusion(f32[1024,4,2,128]{0,3,2,1:T(8,128)} %get-tuple-element.267, f32[4,512,1024,2]{2,1,3,0:T(8,128)S(1)} %get-tuple-element.249, f32[1024,4,2]{0,2,1:T(2,128)S(1)} %fusion.138, pred[1024,512]{0,1:T(8,128)(4,1)S(1)} %compare_or_fusion.2, f32[1024,4,2]{0,2,1:T(2,128)S(1)} %get-tuple-element.251, ...), kind=kOutput, calls=%fused_computation.8.clone.1 | convolution fusion | flops 1097859072 | bytes 26279936 | tf_op jit(solution)/shard_map/while/body/eval_jaxpr/nkgp,pkd->nkgd/dot_general | solution.py:171
  164.4 4.3 %fusion.137 = (f32[1024,4,2]{0,2,1:T(2,128)S(1)}, f32[4,512,1024,2]{2,1,3,0:T(8,128)S(1)}) fusion(pred[1024,512]{0,1:T(8,128)(4,1)S(1)} %compare_or_fusion.2, bf16[1024,4,2,128]{3,0,2,1:T(8,128)(2,1)S(1)} %get-tuple-element.282, bf16[1,512,4,128]{3,2,1,0:T(4,128)(2,1)} %get-tuple-element.247), kind=kOutput, calls=%fused_computation.3.clone.1 | convolution fusion | flops 1086316544 | bytes 19955712 | tf_op jit(solution)/shard_map/while/body/eval_jaxpr/nkgd,pkd->nkgp/dot_general | solution.py:159
  168.8 4.1 fusion.139
  173.0 8.7 %bitcast_add_fusion.2 = f32[1024,4,2,128]{0,3,2,1:T(8,128)} fusion(f32[1024,4,2,128]{0,3,2,1:T(8,128)} %get-tuple-element.267, f32[4,512,1024,2]{2,1,3,0:T(8,128)S(1)} %get-tuple-element.249, f32[1024,4,2]{0,2,1:T(2,128)S(1)} %fusion.138, pred[1024,512]{0,1:T(8,128)(4,1)S(1)} %compare_or_fusion.2, f32[1024,4,2]{0,2,1:T(2,128)S(1)} %get-tuple-element.251, ...), kind=kOutput, calls=%fused_computation.8.clone.1 | convolution fusion | flops 1097859072 | bytes 26279936 | tf_op jit(solution)/shard_map/while/body/eval_jaxpr/nkgp,pkd->nkgd/dot_general | solution.py:171
  185.6 4.3 %fusion.137 = (f32[1024,4,2]{0,2,1:T(2,128)S(1)}, f32[4,512,1024,2]{2,1,3,0:T(8,128)S(1)}) fusion(pred[1024,512]{0,1:T(8,128)(4,1)S(1)} %compare_or_fusion.2, bf16[1024,4,2,128]{3,0,2,1:T(8,128)(2,1)S(1)} %get-tuple-element.282, bf16[1,512,4,128]{3,2,1,0:T(4,128)(2,1)} %get-tuple-element.247), kind=kOutput, calls=%fused_computation.3.clone.1 | convolution fusion | flops 1086316544 | bytes 19955712 | tf_op jit(solution)/shard_map/while/body/eval_jaxpr/nkgd,pkd->nkgp/dot_general | solution.py:159
  190.0 4.1 fusion.139
  194.1 8.7 %bitcast_add_fusion.2 = f32[1024,4,2,128]{0,3,2,1:T(8,128)} fusion(f32[1024,4,2,128]{0,3,2,1:T(8,128)} %get-tuple-element.267, f32[4,512,1024,2]{2,1,3,0:T(8,128)S(1)} %get-tuple-element.249, f32[1024,4,2]{0,2,1:T(2,128)S(1)} %fusion.138, pred[1024,512]{0,1:T(8,128)(4,1)S(1)} %compare_or_fusion.2, f32[1024,4,2]{0,2,1:T(2,128)S(1)} %get-tuple-element.251, ...), kind=kOutput, calls=%fused_computation.8.clone.1 | convolution fusion | flops 1097859072 | bytes 26279936 | tf_op jit(solution)/shard_map/while/body/eval_jaxpr/nkgp,pkd->nkgd/dot_general | solution.py:171
  206.8 4.3 %fusion.137 = (f32[1024,4,2]{0,2,1:T(2,128)S(1)}, f32[4,512,1024,2]{2,1,3,0:T(8,128)S(1)}) fusion(pred[1024,512]{0,1:T(8,128)(4,1)S(1)} %compare_or_fusion.2, bf16[1024,4,2,128]{3,0,2,1:T(8,128)(2,1)S(1)} %get-tuple-element.282, bf16[1,512,4,128]{3,2,1,0:T(4,128)(2,1)} %get-tuple-element.247), kind=kOutput, calls=%fused_computation.3.clone.1 | convolution fusion | flops 1086316544 | bytes 19955712 | tf_op jit(solution)/shard_map/while/body/eval_jaxpr/nkgd,pkd->nkgp/dot_general | solution.py:159
  215.3 8.7 %bitcast_add_fusion.2 = f32[1024,4,2,128]{0,3,2,1:T(8,128)} fusion(f32[1024,4,2,128]{0,3,2,1:T(8,128)} %get-tuple-element.267, f32[4,512,1024,2]{2,1,3,0:T(8,128)S(1)} %get-tuple-element.249, f32[1024,4,2]{0,2,1:T(2,128)S(1)} %fusion.138, pred[1024,512]{0,1:T(8,128)(4,1)S(1)} %compare_or_fusion.2, f32[1024,4,2]{0,2,1:T(2,128)S(1)} %get-tuple-element.251, ...), kind=kOutput, calls=%fused_computation.8.clone.1 | convolution fusion | flops 1097859072 | bytes 26279936 | tf_op jit(solution)/shard_map/while/body/eval_jaxpr/nkgp,pkd->nkgd/dot_general | solution.py:171
  224.0 5.4 %copy.212 = f32[1024,1024]{1,0:T(8,128)} copy(f32[1024,1024]{0,1:T(8,128)} %bitcast.174) | data formatting | bytes 8388608 | tf_op jit(solution)/shard_map/reshape;reshape | solution.py:192
  229.5 57.6 %pmax.7 = bf16[1024,8]{0,1:T(8,128)(2,1)S(1)} all-reduce(bf16[1024,8]{0,1:T(8,128)(2,1)S(1)} %convert_element_type.109), channel_id=1, replica_groups=mesh['kv'=2,'seq'=16] {'seq'}, use_global_device_ids=true, to_apply=%region_13.14 | all-reduce | flops 8192 | bytes 32768 | tf_op jit(solution)/shard_map/pmax | solution.py:190
  298.8 42.2 %reduce-scatter.10.cloned.1.call-done = bf16[64,8]{1,0:T(8,128)(2,1)} async-done(((bf16[1024,8]{1,0:T(8,128)(2,1)}), bf16[64,8]{1,0:T(8,128)(2,1)}) %reduce-scatter.10.cloned.1.call-update) | async-done | bytes 1040
  342.1 63.3 %reduce-scatter.6.cloned.1.call-done = bf16[64,1024]{1,0:T(8,128)(2,1)} async-done(((bf16[1024,1024]{1,0:T(8,128)(2,1)}), bf16[64,1024]{1,0:T(8,128)(2,1)}) %reduce-scatter.6.cloned.1.call-update) | async-done | bytes 131088 | tf_op jit(solution)/shard_map/reduce_scatter | solution.py:196
  410.9 9.8 %reduce-scatter.8.cloned.1.call-done = bf16[64,1024]{1,0:T(8,128)(2,1)} async-done(((bf16[64,2048]{1,0:T(8,128)(2,1)}), bf16[64,1024]{1,0:T(8,128)(2,1)}) %reduce-scatter.8.cloned.1.call-update) | async-done | bytes 131088 | tf_op jit(solution)/shard_map/reduce_scatter | solution.py:219
  (287 shorter events, 70.0 us)
Async XLA Ops:
  7.2 65.7 %copy-start = (bf16[2048,512]{1,0:T(8,128)(2,1)S(1)}, bf16[2048,512]{1,0:T(8,128)(2,1)}, u32[]{:S(2)}) copy-start(bf16[2048,512]{1,0:T(8,128)(2,1)} %param.21) | copy-start | bytes 6291460
  7.2 333.8 %reduce-scatter.10.cloned.1.call-start = ((), (), s32[]{:S(2)}) async-start(), calls=%async_computation.5 | async-start | bytes 278528
  15.5 64.6 %copy-start.4 = (bf16[64,2048]{1,0:T(8,128)(2,1)}, bf16[64,2048]{1,0:T(8,128)(2,1)S(1)}, u32[]{:S(2)}) copy-start(bf16[64,2048]{1,0:T(8,128)(2,1)S(1)} %all_gather.3) | copy-start | bytes 786436
  15.6 57.2 %copy-start.24 = (f32[2048]{0:T(1024)S(1)}, f32[2048]{0:T(1024)}, u32[]{:S(2)}) copy-start(f32[2048]{0:T(1024)} %param.19) | copy-start | bytes 24580
  22.2 50.7 %copy-start.22 = (f32[64,128]{1,0:T(8,128)}, f32[64,128]{1,0:T(8,128)S(1)}, u32[]{:S(2)}) copy-start(f32[64,128]{1,0:T(8,128)S(1)} %pad_maximum_fusion.1) | copy-start | bytes 98308
  22.4 50.3 %copy-start.8 = (f32[64,8,64]{2,0,1:T(8,128)}, f32[64,8,64]{2,0,1:T(8,128)S(1)}, u32[]{:S(2)}) copy-start(f32[64,8,64]{2,0,1:T(8,128)S(1)} %get-tuple-element.168) | copy-start | bytes 393220
  22.4 50.4 %copy-start.10 = (f32[64,8,64]{2,0,1:T(8,128)}, f32[64,8,64]{2,0,1:T(8,128)S(1)}, u32[]{:S(2)}) copy-start(f32[64,8,64]{2,0,1:T(8,128)S(1)} %get-tuple-element.169) | copy-start | bytes 393220
  23.1 7.1 %collective-permute-start = (bf16[64,1024]{1,0:T(8,128)(2,1)S(1)}, bf16[64,1024]{1,0:T(8,128)(2,1)S(1)}, u32[]{:S(2)}, u32[]{:S(2)}) collective-permute-start(bf16[64,1024]{1,0:T(8,128)(2,1)S(1)} %fusion.35), channel_id=1, source_target_pairs={{0,1},{1,2},{2,3},{3,4},{4,5},{5,6},{6,7},{7,8},{8,9},{9,10},{10,1... | collective-permute-start | bytes 393224 | tf_op jit(solution)/shard_map/ppermute | solution.py:142
  30.2 7.1 %collective-permute-start.1 = (bf16[64,1024]{1,0:T(8,128)(2,1)S(1)}, bf16[64,1024]{1,0:T(8,128)(2,1)S(1)}, u32[]{:S(2)}, u32[]{:S(2)}) collective-permute-start(bf16[64,1024]{1,0:T(8,128)(2,1)S(1)} %collective-permute-done), channel_id=1, source_target_pairs={{0,1},{1,2},{2,3},{3,4},{4,5},{5,6},{6,7},{7,8},{8,9},{9,10},{10,1... | collective-permute-start | bytes 393224 | tf_op jit(solution)/shard_map/ppermute | solution.py:142
  37.3 7.1 %collective-permute-start.2 = (bf16[64,1024]{1,0:T(8,128)(2,1)S(1)}, bf16[64,1024]{1,0:T(8,128)(2,1)S(1)}, u32[]{:S(2)}, u32[]{:S(2)}) collective-permute-start(bf16[64,1024]{1,0:T(8,128)(2,1)S(1)} %collective-permute-done.1), channel_id=1, source_target_pairs={{0,1},{1,2},{2,3},{3,4},{4,5},{5,6},{6,7},{7,8},{8,9},{9,10},{10,1... | collective-permute-start | bytes 393224 | tf_op jit(solution)/shard_map/ppermute | solution.py:142
  44.4 7.1 %collective-permute-start.3 = (bf16[64,1024]{1,0:T(8,128)(2,1)S(1)}, bf16[64,1024]{1,0:T(8,128)(2,1)S(1)}, u32[]{:S(2)}, u32[]{:S(2)}) collective-permute-start(bf16[64,1024]{1,0:T(8,128)(2,1)S(1)} %collective-permute-done.2), channel_id=1, source_target_pairs={{0,1},{1,2},{2,3},{3,4},{4,5},{5,6},{6,7},{7,8},{8,9},{9,10},{10,1... | collective-permute-start | bytes 393224 | tf_op jit(solution)/shard_map/ppermute | solution.py:142
  51.5 7.1 %collective-permute-start.4 = (bf16[64,1024]{1,0:T(8,128)(2,1)S(1)}, bf16[64,1024]{1,0:T(8,128)(2,1)S(1)}, u32[]{:S(2)}, u32[]{:S(2)}) collective-permute-start(bf16[64,1024]{1,0:T(8,128)(2,1)S(1)} %collective-permute-done.3), channel_id=1, source_target_pairs={{0,1},{1,2},{2,3},{3,4},{4,5},{5,6},{6,7},{7,8},{8,9},{9,10},{10,1... | collective-permute-start | bytes 393224 | tf_op jit(solution)/shard_map/ppermute | solution.py:142
  58.6 7.1 %collective-permute-start.5 = (bf16[64,1024]{1,0:T(8,128)(2,1)S(1)}, bf16[64,1024]{1,0:T(8,128)(2,1)S(1)}, u32[]{:S(2)}, u32[]{:S(2)}) collective-permute-start(bf16[64,1024]{1,0:T(8,128)(2,1)S(1)} %collective-permute-done.4), channel_id=1, source_target_pairs={{0,1},{1,2},{2,3},{3,4},{4,5},{5,6},{6,7},{7,8},{8,9},{9,10},{10,1... | collective-permute-start | bytes 393224 | tf_op jit(solution)/shard_map/ppermute | solution.py:142
  65.7 7.1 %collective-permute-start.6 = (bf16[64,1024]{1,0:T(8,128)(2,1)S(1)}, bf16[64,1024]{1,0:T(8,128)(2,1)S(1)}, u32[]{:S(2)}, u32[]{:S(2)}) collective-permute-start(bf16[64,1024]{1,0:T(8,128)(2,1)S(1)} %collective-permute-done.5), channel_id=1, source_target_pairs={{0,1},{1,2},{2,3},{3,4},{4,5},{5,6},{6,7},{7,8},{8,9},{9,10},{10,1... | collective-permute-start | bytes 393224 | tf_op jit(solution)/shard_map/ppermute | solution.py:142
  72.8 42.9 %copy-start.17 = (bf16[64,1024]{1,0:T(8,128)(2,1)}, bf16[64,1024]{1,0:T(8,128)(2,1)S(1)}, u32[]{:S(2)}) copy-start(bf16[64,1024]{1,0:T(8,128)(2,1)S(1)} %collective-permute-done.6) | copy-start | bytes 393220
  72.8 7.2 %collective-permute-start.7 = (bf16[64,1024]{1,0:T(8,128)(2,1)S(1)}, bf16[64,1024]{1,0:T(8,128)(2,1)}, u32[]{:S(2)}, u32[]{:S(2)}) collective-permute-start(bf16[64,1024]{1,0:T(8,128)(2,1)S(1)} %collective-permute-done.6), channel_id=1, source_target_pairs={{0,1},{1,2},{2,3},{3,4},{4,5},{5,6},{6,7},{7,8},{8,9},{9,10},{10,1... | collective-permute-start | bytes 393224 | tf_op jit(solution)/shard_map/ppermute | solution.py:142
  74.1 60.8 %copy-start.6 = (f32[64,512]{1,0:T(8,128)}, f32[64,512]{1,0:T(8,128)S(1)}, u32[]{:S(2)}) copy-start(f32[64,512]{1,0:T(8,128)S(1)} %fusion.94) | copy-start | bytes 393220
  74.1 60.7 %copy-start.16 = (bf16[64,1024]{1,0:T(8,128)(2,1)S(1)}, bf16[64,1024]{1,0:T(8,128)(2,1)}, u32[]{:S(2)}) copy-start(bf16[64,1024]{1,0:T(8,128)(2,1)} %copy-done.15) | copy-start | bytes 393220
  74.1 60.8 %copy-start.14 = (bf16[64,1024]{1,0:T(8,128)(2,1)S(1)}, bf16[64,1024]{1,0:T(8,128)(2,1)}, u32[]{:S(2)}) copy-start(bf16[64,1024]{1,0:T(8,128)(2,1)} %copy-done.13) | copy-start | bytes 393220
  80.0 7.3 %collective-permute-start.8 = (bf16[64,1024]{1,0:T(8,128)(2,1)}, bf16[64,1024]{1,0:T(8,128)(2,1)S(1)}, u32[]{:S(2)}, u32[]{:S(2)}) collective-permute-start(bf16[64,1024]{1,0:T(8,128)(2,1)} %collective-permute-done.7), channel_id=1, source_target_pairs={{0,1},{1,2},{2,3},{3,4},{4,5},{5,6},{6,7},{7,8},{8,9},{9,10},{10,1... | collective-permute-start | bytes 393224 | tf_op jit(solution)/shard_map/ppermute | solution.py:142
  87.3 7.1 %collective-permute-start.9 = (bf16[64,1024]{1,0:T(8,128)(2,1)S(1)}, bf16[64,1024]{1,0:T(8,128)(2,1)S(1)}, u32[]{:S(2)}, u32[]{:S(2)}) collective-permute-start(bf16[64,1024]{1,0:T(8,128)(2,1)S(1)} %collective-permute-done.8), channel_id=1, source_target_pairs={{0,1},{1,2},{2,3},{3,4},{4,5},{5,6},{6,7},{7,8},{8,9},{9,10},{10,1... | collective-permute-start | bytes 393224 | tf_op jit(solution)/shard_map/ppermute | solution.py:142
  94.4 7.1 %collective-permute-start.10 = (bf16[64,1024]{1,0:T(8,128)(2,1)S(1)}, bf16[64,1024]{1,0:T(8,128)(2,1)S(1)}, u32[]{:S(2)}, u32[]{:S(2)}) collective-permute-start(bf16[64,1024]{1,0:T(8,128)(2,1)S(1)} %collective-permute-done.9), channel_id=1, source_target_pairs={{0,1},{1,2},{2,3},{3,4},{4,5},{5,6},{6,7},{7,8},{8,9},{9,10},{10,1... | collective-permute-start | bytes 393224 | tf_op jit(solution)/shard_map/ppermute | solution.py:142
  101.5 7.1 %collective-permute-start.11 = (bf16[64,1024]{1,0:T(8,128)(2,1)S(1)}, bf16[64,1024]{1,0:T(8,128)(2,1)S(1)}, u32[]{:S(2)}, u32[]{:S(2)}) collective-permute-start(bf16[64,1024]{1,0:T(8,128)(2,1)S(1)} %collective-permute-done.10), channel_id=1, source_target_pairs={{0,1},{1,2},{2,3},{3,4},{4,5},{5,6},{6,7},{7,8},{8,9},{9,10},{10,1... | collective-permute-start | bytes 393224 | tf_op jit(solution)/shard_map/ppermute | solution.py:142
  108.6 7.1 %collective-permute-start.12 = (bf16[64,1024]{1,0:T(8,128)(2,1)S(1)}, bf16[64,1024]{1,0:T(8,128)(2,1)S(1)}, u32[]{:S(2)}, u32[]{:S(2)}) collective-permute-start(bf16[64,1024]{1,0:T(8,128)(2,1)S(1)} %collective-permute-done.11), channel_id=1, source_target_pairs={{0,1},{1,2},{2,3},{3,4},{4,5},{5,6},{6,7},{7,8},{8,9},{9,10},{10,1... | collective-permute-start | bytes 393224 | tf_op jit(solution)/shard_map/ppermute | solution.py:142
  115.7 7.1 %collective-permute-start.13 = (bf16[64,1024]{1,0:T(8,128)(2,1)S(1)}, bf16[64,1024]{1,0:T(8,128)(2,1)S(1)}, u32[]{:S(2)}, u32[]{:S(2)}) collective-permute-start(bf16[64,1024]{1,0:T(8,128)(2,1)S(1)} %collective-permute-done.12), channel_id=1, source_target_pairs={{0,1},{1,2},{2,3},{3,4},{4,5},{5,6},{6,7},{7,8},{8,9},{9,10},{10,1... | collective-permute-start | bytes 393224 | tf_op jit(solution)/shard_map/ppermute | solution.py:142
  115.7 19.1 %copy-start.18 = (bf16[64,1024]{1,0:T(8,128)(2,1)S(1)}, bf16[64,1024]{1,0:T(8,128)(2,1)}, u32[]{:S(2)}) copy-start(bf16[64,1024]{1,0:T(8,128)(2,1)} %copy-done.17) | copy-start | bytes 393220
  122.8 7.1 %collective-permute-start.14 = (bf16[64,1024]{1,0:T(8,128)(2,1)S(1)}, bf16[64,1024]{1,0:T(8,128)(2,1)S(1)}, u32[]{:S(2)}, u32[]{:S(2)}) collective-permute-start(bf16[64,1024]{1,0:T(8,128)(2,1)S(1)} %collective-permute-done.13), channel_id=1, source_target_pairs={{0,1},{1,2},{2,3},{3,4},{4,5},{5,6},{6,7},{7,8},{8,9},{9,10},{10,1... | collective-permute-start | bytes 393224 | tf_op jit(solution)/shard_map/ppermute | solution.py:142
  288.1 117.3 %reduce-scatter.6.cloned.1.call-start = ((), (), s32[]{:S(2)}) async-start(), calls=%async_computation.3 | async-start | bytes 2228224 | tf_op jit(solution)/shard_map/reduce_scatter | solution.py:196
  292.8 127.9 %reduce-scatter.8.cloned.1.call-start = ((), (), s32[]{:S(2)}) async-start(), calls=%async_computation.4 | async-start | bytes 393216 | tf_op jit(solution)/shard_map/reduce_scatter | solution.py:219
  298.3 111.6 %copy-start.30 = (f32[2,32]{1,0:T(2,128)S(1)}, f32[2,32]{1,0:T(2,128)}, u32[]{:S(2)}) copy-start(f32[2,32]{1,0:T(2,128)} %get-tuple-element.176) | copy-start | bytes 772
  298.8 121.9 %copy-start.12 = (bf16[64,1024]{1,0:T(8,128)(2,1)S(1)}, bf16[64,1024]{1,0:T(8,128)(2,1)}, u32[]{:S(2)}) copy-start(bf16[64,1024]{1,0:T(8,128)(2,1)} %param.18) | copy-start | bytes 393220
  341.9 80.4 %copy-start.1 = (bf16[2048,512]{1,0:T(8,128)(2,1)S(1)}, bf16[2048,512]{1,0:T(8,128)(2,1)}, u32[]{:S(2)}) copy-start(bf16[2048,512]{1,0:T(8,128)(2,1)} %param.21) | copy-start | bytes 6291460
  (30 other events, 177.9 us)
Sparse Core Ops, SparseCore 0:
  288.2 52.7 reduce-scatter.9
  344.8 60.6 reduce-scatter.5
  410.0 10.6 reduce-scatter.7
